TPU v7x, 32 devices: a whole 2x2x4 slice. The times are simulated.
32 devices in a mesh: tensor: 2 (over y), context: 16 (over z, x, core).
Axes of the slice: x: 2, y: 2, z: 4, core: 2. Of those that a mesh axis runs over, the one named last changes fastest.
Arguments:
- query_stream: bfloat16 [8192, 2048], P('tensor', 'context'), may hold values from -6 to 6
- key_stream: bfloat16 [8192, 2048], P('tensor', 'context'), may hold values from -6 to 6
- value_stream: bfloat16 [8192, 2048], P('tensor', 'context'), may hold values from -6 to 6
- filter_taps: bfloat16 [2048, 8192], P(('tensor', 'context')), may hold values from -0.125 to 0.125
- short_filters: float32 [3, 3, 8192], P(None, None, ('tensor', 'context')), may hold values from -3 to 3
- skip_gain: float32 [8192], P(('tensor', 'context')), may hold values from 0.5 to 1.5
Outputs:
- gated_out: bfloat16 [8192, 2048], P('tensor', 'context')
All inputs are finite; a program needn't handle non-finite values.
Results may differ from a plain program's by a relative error of at most 0.0057.
Values may be sent and summed in bfloat16 or wider, within the bound.
A program may use at most 128 MiB of HBM per device.

v0:
```python
import math
import jax
import jax.numpy as jnp
from jax import lax
from jax.sharding import PartitionSpec as P

HIGHEST = lax.Precision.HIGHEST
THREEPASS = lax.Precision.HIGH
first_order = 128


def shifted(value, axis, steps):
    count = lax.axis_size(axis)
    initial, last = (max(0, -steps), min(count, count - steps))
    return lax.ppermute(value, axis, [(source, source + steps) for source in range(initial, last)])


def unit_tables(size_left, size_right, modulus):
    index_left = jnp.arange(size_left, dtype=jnp.int32)
    index_right = jnp.arange(size_right, dtype=jnp.int32)
    phases = (index_left[:, None] * index_right[None, :] % modulus).astype(jnp.float32)
    radians = phases * (2.0 * math.pi / modulus)
    return (jnp.cos(radians), -jnp.sin(radians))


def short_filter(signal, weights, before):
    joined = jnp.concatenate([before, signal], axis=1)
    length = signal.shape[1]
    return (
        weights[0][:, None] * joined[:, 2:]
        + weights[1][:, None] * joined[:, 1 : length + 1]
        + weights[2][:, None] * joined[:, :length]
    )


def causal_mix(inputs, filters):
    channels, length = inputs.shape
    modulus = 2 * length
    second = modulus // first_order
    half_rows = first_order // 2
    first_cos, first_sin = unit_tables(first_order, first_order, first_order)
    second_cos, second_sin = unit_tables(second, second, second)
    twist_cos, twist_sin = unit_tables(first_order, second, modulus)
    head_cos = first_cos[:, :half_rows]
    head_sin = first_sin[:, :half_rows]

    def forward(signal):
        shaped = signal.reshape(channels, half_rows, second)
        part_real = jnp.einsum("kn,cnm->ckm", head_cos, shaped, precision=THREEPASS)
        part_imag = jnp.einsum("kn,cnm->ckm", head_sin, shaped, precision=THREEPASS)
        turn_real = part_real * twist_cos - part_imag * twist_sin
        turn_imag = part_real * twist_sin + part_imag * twist_cos
        out_real = jnp.einsum("ckm,mj->ckj", turn_real, second_cos, precision=HIGHEST) - jnp.einsum(
            "ckm,mj->ckj", turn_imag, second_sin, precision=HIGHEST
        )
        out_imag = jnp.einsum("ckm,mj->ckj", turn_real, second_sin, precision=HIGHEST) + jnp.einsum(
            "ckm,mj->ckj", turn_imag, second_cos, precision=HIGHEST
        )
        return (out_real, out_imag)

    input_real, input_imag = forward(inputs)
    filter_real, filter_imag = forward(filters)
    product_real = input_real * filter_real - input_imag * filter_imag
    product_imag = input_real * filter_imag + input_imag * filter_real
    back_real = jnp.einsum("ckm,mj->ckj", product_real, second_cos, precision=HIGHEST) + jnp.einsum(
        "ckm,mj->ckj", product_imag, second_sin, precision=HIGHEST
    )
    back_imag = jnp.einsum("ckm,mj->ckj", product_imag, second_cos, precision=HIGHEST) - jnp.einsum(
        "ckm,mj->ckj", product_real, second_sin, precision=HIGHEST
    )
    untwist_real = back_real * twist_cos + back_imag * twist_sin
    untwist_imag = back_imag * twist_cos - back_real * twist_sin
    result = jnp.einsum(
        "nk,ckm->cnm", first_cos[:half_rows, :], untwist_real, precision=HIGHEST
    ) + jnp.einsum("nk,ckm->cnm", first_sin[:half_rows, :], untwist_imag, precision=HIGHEST)
    return (result / modulus).reshape(channels, length)


def local(query_stream, key_stream, value_stream, filter_taps, short_filters, skip_gain):
    group_width, block_rows = query_stream.shape
    context_size = lax.axis_size("context")
    tensor_size = lax.axis_size("tensor")
    local_channels = group_width // context_size
    offset_rows = filter_taps.shape[0]
    laid_out = filter_taps.reshape(offset_rows, tensor_size, context_size, local_channels)
    arrived_taps = lax.all_to_all(laid_out, "tensor", split_axis=1, concat_axis=0, tiled=True)
    arrived_taps = lax.all_to_all(arrived_taps, "context", split_axis=2, concat_axis=0, tiled=True)
    filters = arrived_taps.reshape(context_size, tensor_size, offset_rows, local_channels)
    filters = filters.transpose(3, 1, 0, 2).reshape(local_channels, -1)
    filters = filters.astype(jnp.float32)
    weights = lax.all_gather(short_filters, "context", axis=2, tiled=True)
    rim_cols = shifted(jnp.stack([query_stream, key_stream, value_stream])[:, :, -2:], "context", 1)
    rim_cols = rim_cols.astype(jnp.float32)
    query_short = short_filter(query_stream.astype(jnp.float32), weights[0], rim_cols[0])
    key_short = short_filter(key_stream.astype(jnp.float32), weights[1], rim_cols[1])
    value_short = short_filter(value_stream.astype(jnp.float32), weights[2], rim_cols[2])
    products = (key_short * value_short).astype(jnp.bfloat16)
    arrived = lax.all_to_all(
        products.reshape(context_size, local_channels, block_rows),
        "context",
        split_axis=0,
        concat_axis=2,
        tiled=True,
    )
    arrived = arrived[0].astype(jnp.float32)
    convolved = causal_mix(arrived, filters)
    mixed_out = (convolved + skip_gain[:, None] * arrived).astype(jnp.bfloat16)
    returned = lax.all_to_all(mixed_out[None], "context", split_axis=2, concat_axis=0, tiled=True)
    returned = returned.reshape(group_width, block_rows)
    return (query_short * returned.astype(jnp.float32)).astype(jnp.bfloat16)


def solution(mesh):
    placed = (
        P("tensor", "context"),
        P("tensor", "context"),
        P("tensor", "context"),
        P(("tensor", "context"), None),
        P(None, None, ("tensor", "context")),
        P(("tensor", "context")),
    )
    return jax.shard_map(
        local, mesh=mesh, in_specs=placed, out_specs=P("tensor", "context"), check_vma=False
    )
```

profile of v0, /device:TPU:13, one launch (start us, length us, event | category | flops | bytes accessed | tf_op | source)
XLA Modules:
  0.0 307.0 jit_solution(17208289329332975849)
XLA Ops:
  16.3 18.4 %all_gather.3 = f32[3,3,4096]{2,1,0:T(4,128)S(1)} all-gather(f32[3,3,256]{2,1,0:T(4,128)S(1)} %copy-done.12), channel_id=1, replica_groups=mesh['tensor'=2,'context'=16] {'context'}, dimensions={2}, use_global_device_ids=true | all-gather | bytes 156672 | tf_op jit(solution)/shard_map/all_gather | solution.py:91
  42.7 7.9 %fusion.29 = bf16[4096,128]{1,0:T(8,128)(2,1)} fusion(f32[4096,2]{1,0:T(8,128)S(1)} %get-tuple-element.12, f32[4096,128]{1,0:T(8,128)S(1)} %copy-done.8, f32[4096,2]{1,0:T(8,128)S(1)} %get-tuple-element.11, f32[4096,128]{1,0:T(8,128)S(1)} %copy-done.7, f32[4096]{0:T(1024)S(1)} %bitcast.149, f32[4096]{0:T(1024)S(1)} %bitcast.150, f32[4096]{0:T(1024)S(1)} %bitcast.151, ...), kind=kLoop, calls=%fused_computation.43 | loop fusion | flops 8388608 | bytes 5406720 | tf_op jit(solution)/shard_map/convert_element_type | solution.py:97
  50.6 6.5 %all-to-all-start = ((bf16[16,256,128]{2,1,0:T(8,128)(2,1)}), bf16[16,256,128]{2,1,0:T(8,128)(2,1)S(1)}, u32[]{:S(2)}, u32[]{:S(2)}) async-start(bf16[16,256,128]{2,1,0:T(8,128)(2,1)} %bitcast.15), calls=%async_computation | async-start | bytes 2097152 | tf_op jit(solution)/shard_map/all_to_all | solution.py:98
  60.3 21.7 %all-to-all-done = bf16[16,256,128]{2,1,0:T(8,128)(2,1)S(1)} async-done(((bf16[16,256,128]{2,1,0:T(8,128)(2,1)}), bf16[16,256,128]{2,1,0:T(8,128)(2,1)S(1)}, u32[]{:S(2)}, u32[]{:S(2)}) %all-to-all-start) | async-done | bytes 1048608 | tf_op jit(solution)/shard_map/all_to_all | solution.py:98
  82.0 5.3 %all-to-all-start.2 = ((bf16[128,1,16,256]{3,0,1,2:T(8,128)(2,1)}), bf16[128,1,16,256]{3,0,1,2:T(8,128)(2,1)S(1)}, u32[]{:S(2)}, u32[]{:S(2)}) async-start(bf16[128,1,16,256]{3,0,1,2:T(8,128)(2,1)} %copy.105), calls=%async_computation.2 | async-start | bytes 2097152 | tf_op jit(solution)/shard_map/all_to_all | solution.py:87
  96.7 6.4 %fusion.12 = f32[256,128,32]{1,2,0:T(8,128)S(1)} fusion(f32[256,128,32]{1,0,2:T(8,128)S(1)} %get-tuple-element.10), kind=kOutput, calls=%fused_computation.28 | convolution fusion | flops 402668544 | bytes 8388608 | tf_op jit(solution)/shard_map/ckm,mj->ckj/dot_general | solution.py:53
  103.1 9.1 %fusion.10 = f32[256,128,32]{1,2,0:T(8,128)} fusion(f32[256,128,32]{1,0,2:T(8,128)S(1)} %get-tuple-element.10), kind=kOutput, calls=%fused_computation.26 | convolution fusion | flops 402667520 | bytes 8388608 | tf_op jit(solution)/shard_map/ckm,mj->ckj/dot_general | solution.py:56
  112.1 8.9 %fusion.18 = f32[256,128,32]{1,2,0:T(8,128)} fusion(f32[256,128,32]{1,2,0:T(8,128)S(1)} %fusion.12, f32[256,128,32]{1,0,2:T(8,128)S(1)} %get-tuple-element.9), kind=kOutput, calls=%fused_computation.34 | convolution fusion | flops 403716096 | bytes 12582912 | tf_op jit(solution)/shard_map/ckm,mj->ckj/dot_general | solution.py:53
  122.7 5.7 %add_bitcast_fusion = (f32[256,128,32]{0,1,2:T(8,128)}, f32[256,128,32]{0,1,2:T(8,128)}) fusion(f32[128,256,32]{1,0,2:T(8,128)S(1)} %fusion.51, f32[128,32]{0,1:T(8,128)S(1)} %get-tuple-element.23, f32[128,32]{0,1:T(8,128)S(1)} %get-tuple-element.24, bf16[256,64,32]{0,2,1:T(8,128)(2,1)S(1)} %bitcast.136, f32[128,128]{0,1:T(8,128)S(1)} %fusion.65), kind=kOutput, calls=%fused_computation.24 | convolution fusion | flops 408944640 | bytes 13697024 | tf_op jit(solution)/shard_map/kn,cnm->ckm/dot_general | solution.py:49
  128.3 5.8 %copy.109 = f32[256,128,32]{1,2,0:T(8,128)} copy(f32[256,128,32]{0,1,2:T(8,128)} %get-tuple-element.8) | data formatting | bytes 8388608 | tf_op jit(solution)/shard_map/sub | solution.py:51
  134.2 8.0 %fusion.76 = f32[256,128,32]{1,2,0:T(8,128)} fusion(f32[256,128,32]{1,2,0:T(8,128)} %copy.109), kind=kOutput, calls=%fused_computation.113 | convolution fusion | flops 402668544 | bytes 8388608 | tf_op jit(solution)/shard_map/ckm,mj->ckj/dot_general | solution.py:56
  142.2 5.4 %fusion.87 = f32[256,128,32]{1,2,0:T(8,128)} fusion(f32[256,128,32]{1,2,0:T(8,128)S(1)} %copy-done.3), kind=kOutput, calls=%fused_computation.124 | convolution fusion | flops 402667520 | bytes 8388608 | tf_op jit(solution)/shard_map/ckm,mj->ckj/dot_general | solution.py:53
  147.5 5.5 %copy.110 = f32[256,128,32]{1,2,0:T(8,128)} copy(f32[256,128,32]{0,1,2:T(8,128)} %get-tuple-element.7) | data formatting | bytes 8388608 | tf_op jit(solution)/shard_map/add | solution.py:52
  153.0 7.7 %convolution_add_fusion = f32[256,128,32]{1,2,0:T(8,128)S(1)} fusion(f32[256,128,32]{1,2,0:T(8,128)} %fusion.76, f32[256,128,32]{1,2,0:T(8,128)} %copy.110), kind=kOutput, calls=%fused_computation.36 | convolution fusion | flops 403716096 | bytes 12582912 | tf_op jit(solution)/shard_map/ckm,mj->ckj/dot_general | solution.py:56
  160.8 5.3 %convolution_subtract_fusion = f32[256,128,32]{1,2,0:T(8,128)} fusion(f32[256,128,32]{1,2,0:T(8,128)S(1)} %copy-done.5, f32[256,128,32]{1,2,0:T(8,128)S(1)} %copy-done.2), kind=kOutput, calls=%fused_computation.37 | convolution fusion | flops 403717120 | bytes 12582912 | tf_op jit(solution)/shard_map/ckm,mj->ckj/dot_general | solution.py:53
  166.1 11.6 %multiply_subtract_fusion = (f32[256,128,32]{1,2,0:T(8,128)S(1)}, f32[256,128,32]{1,2,0:T(8,128)S(1)}) fusion(f32[256,128,32]{1,2,0:T(8,128)S(1)} %convolution_add_fusion, f32[256,128,32]{1,2,0:T(8,128)S(1)} %copy-done.4, f32[256,128,32]{1,2,0:T(8,128)} %convolution_subtract_fusion, f32[256,128,32]{1,2,0:T(8,128)} %fusion.10, f32[256,128,32]{1,0,2:T(8,128)S(1)} %copy-done.1), kind=kOutput, calls=%fused_computation.23 | convolution fusion | flops 410008576 | bytes 29360128 | tf_op jit(solution)/shard_map/ckm,mj->ckj/dot_general | solution.py:56
  194.1 17.6 %fusion.2 = f32[256,32,64]{0,2,1:T(8,128)S(1)} fusion(f32[128,32]{0,1:T(8,128)S(1)} %get-tuple-element.23, f32[128,32]{0,1:T(8,128)S(1)} %get-tuple-element.24, f32[256,128,32]{1,2,0:T(8,128)S(1)} %fusion.74, f32[256,128,32]{1,2,0:T(8,128)S(1)} %fusion.83, f32[256,128,32]{1,2,0:T(8,128)S(1)} %fusion.72, f32[256,128,32]{1,2,0:T(8,128)S(1)} %fusion.81, ...), kind=kOutput, calls=%fused_computation.14 | convolution fusion | flops 810549248 | bytes 18972672 | tf_op jit(solution)/shard_map/nk,ckm->cnm/dot_general | solution.py:75
  211.8 17.6 %multiply_bitcast_fusion = f32[256,64,32]{0,1,2:T(8,128)S(1)} fusion(f32[256,32,64]{0,2,1:T(8,128)S(1)} %fusion.2, f32[128,32]{0,1:T(8,128)S(1)} %get-tuple-element.23, f32[128,32]{0,1:T(8,128)S(1)} %get-tuple-element.24, f32[256,128,32]{1,2,0:T(8,128)S(1)} %fusion.74, f32[256,128,32]{1,2,0:T(8,128)S(1)} %fusion.83, f32[256,128,32]{1,2,0:T(8,128)S(1)} %fusion.72, ...), kind=kOutput, calls=%fused_computation.67 | convolution fusion | flops 811597824 | bytes 21069824 | tf_op jit(solution)/shard_map/nk,ckm->cnm/dot_general | solution.py:73
  231.4 11.7 %copy.186 = bf16[1,256,2048]{1,0,2:T(2,128)(2,1)S(1)} copy(bf16[1,256,2048]{1,2,0:T(8,128)(2,1)S(1)} %fusion.44) | data formatting | bytes 2097152 | tf_op jit(solution)/shard_map/convert_element_type | solution.py:107
  243.7 11.5 %reduce = bf16[2048,256]{1,0:T(8,128)(2,1)} reduce(bf16[2048,1,256]{2,1,0:T(2,128)(2,1)S(1)} %bitcast.138, bf16[]{:T(256)} %broadcast.146), dimensions={1}, to_apply=%bitcast.131.reduce_sub_computation | reduce | bytes 2097154
  257.3 6.0 %all-to-all-start.3 = ((bf16[16,2,16384]{2,1,0:T(2,128)(2,1)}), bf16[16,2,16384]{2,1,0:T(2,128)(2,1)}, u32[]{:S(2)}, u32[]{:S(2)}) async-start(bf16[16,2,16384]{2,1,0:T(2,128)(2,1)} %reshape.154), calls=%async_computation.3 | async-start | bytes 2097152 | tf_op jit(solution)/shard_map/all_to_all | solution.py:108
  263.5 24.9 %all-to-all-done.3 = bf16[16,2,16384]{2,1,0:T(2,128)(2,1)} async-done(((bf16[16,2,16384]{2,1,0:T(2,128)(2,1)}), bf16[16,2,16384]{2,1,0:T(2,128)(2,1)}, u32[]{:S(2)}, u32[]{:S(2)}) %all-to-all-start.3) | async-done | bytes 1048608 | tf_op jit(solution)/shard_map/all_to_all | solution.py:108
  288.4 5.8 %reshape.155 = bf16[2048,1,256]{2,1,0:T(2,128)(2,1)} reshape(bf16[16,2,16384]{2,1,0:T(2,128)(2,1)} %all-to-all-done.3) | data formatting | bytes 2097152
  300.3 6.4 %fusion.39 = bf16[4096,128]{1,0:T(8,128)(2,1)} fusion(f32[4096,2]{1,0:T(8,128)} %get-tuple-element.13, f32[4096,128]{1,0:T(8,128)S(1)} %convert_element_type.124, f32[16,1,256,128]{3,2,0,1:T(8,128)} %copy.125, f32[4096]{0:T(1024)S(1)} %bitcast.147, f32[4096]{0:T(1024)S(1)} %bitcast.148, f32[4096]{0:T(1024)S(1)} %bitcast.146), kind=kLoop, calls=%fused_computation.53 | loop fusion | flops 4718592 | bytes 5324800 | tf_op jit(solution)/shard_map/convert_element_type | solution.py:110
  (68 shorter events, 65.8 us)
Async XLA Ops:
  0.0 3.1 %copy-start.10 = (bf16[4096,128]{1,0:T(8,128)(2,1)S(1)}, bf16[4096,128]{1,0:T(8,128)(2,1)}, u32[]{:S(2)}) copy-start(bf16[4096,128]{1,0:T(8,128)(2,1)} %param.8) | copy-start | bytes 3145732
  4.4 11.9 %copy-start.12 = (f32[3,3,256]{2,1,0:T(4,128)S(1)}, f32[3,3,256]{2,1,0:T(4,128)}, u32[]{:S(2)}) copy-start(f32[3,3,256]{2,1,0:T(4,128)} %param.10) | copy-start | bytes 27652
  5.3 29.5 %copy-start.9 = (bf16[4096,128]{1,0:T(8,128)(2,1)S(1)}, bf16[4096,128]{1,0:T(8,128)(2,1)}, u32[]{:S(2)}) copy-start(bf16[4096,128]{1,0:T(8,128)(2,1)} %param.7) | copy-start | bytes 3145732
  5.3 32.4 %collective-permute-start = (bf16[3,4096,2]{1,2,0:T(2,128)(2,1)S(1)}, bf16[3,4096,2]{1,2,0:T(2,128)(2,1)S(1)}, u32[]{:S(2)}, u32[]{:S(2)}) collective-permute-start(bf16[3,4096,2]{1,2,0:T(2,128)(2,1)S(1)} %pad_maximum_fusion.3), channel_id=1, source_target_pairs={{0,1},{1,2},{2,3},{3,4},{4,5},{5,6},{6,7},{7,8},{8,9},{9,10},{10,1... | collective-permute-start | bytes 147464 | tf_op jit(solution)/shard_map/ppermute | solution.py:15
  11.7 38.9 %all-to-all-start.1 = ((bf16[64,2,16,256]{3,2,0,1:T(8,128)(2,1)}), bf16[64,2,16,256]{3,2,0,1:T(8,128)(2,1)}, u32[]{:S(2)}, u32[]{:S(2)}) async-start(bf16[64,2,16,256]{3,2,0,1:T(8,128)(2,1)} %copy.104), calls=%async_computation.1 | async-start | bytes 2097152 | tf_op jit(solution)/shard_map/all_to_all | solution.py:86
  39.7 2.1 copy-start.7
  39.7 3.0 copy-start.8
  50.6 31.5 %all-to-all-start = ((bf16[16,256,128]{2,1,0:T(8,128)(2,1)}), bf16[16,256,128]{2,1,0:T(8,128)(2,1)S(1)}, u32[]{:S(2)}, u32[]{:S(2)}) async-start(bf16[16,256,128]{2,1,0:T(8,128)(2,1)} %bitcast.15), calls=%async_computation | async-start | bytes 2097152 | tf_op jit(solution)/shard_map/all_to_all | solution.py:98
  82.0 39.0 %all-to-all-start.2 = ((bf16[128,1,16,256]{3,0,1,2:T(8,128)(2,1)}), bf16[128,1,16,256]{3,0,1,2:T(8,128)(2,1)S(1)}, u32[]{:S(2)}, u32[]{:S(2)}) async-start(bf16[128,1,16,256]{3,0,1,2:T(8,128)(2,1)} %copy.105), calls=%async_computation.2 | async-start | bytes 2097152 | tf_op jit(solution)/shard_map/all_to_all | solution.py:87
  96.7 15.4 %copy-start = (f32[256,128,32]{1,0,2:T(8,128)}, f32[256,128,32]{1,0,2:T(8,128)S(1)}, u32[]{:S(2)}) copy-start(f32[256,128,32]{1,0,2:T(8,128)S(1)} %get-tuple-element.9) | copy-start | bytes 12582916
  134.2 8.0 %copy-start.3 = (f32[256,128,32]{1,2,0:T(8,128)S(1)}, f32[256,128,32]{1,2,0:T(8,128)}, u32[]{:S(2)}) copy-start(f32[256,128,32]{1,2,0:T(8,128)} %copy.109) | copy-start | bytes 12582916
  153.0 7.7 %copy-start.2 = (f32[256,128,32]{1,2,0:T(8,128)S(1)}, f32[256,128,32]{1,2,0:T(8,128)}, u32[]{:S(2)}) copy-start(f32[256,128,32]{1,2,0:T(8,128)} %copy.110) | copy-start | bytes 12582916
  153.0 7.7 %copy-start.5 = (f32[256,128,32]{1,2,0:T(8,128)S(1)}, f32[256,128,32]{1,2,0:T(8,128)}, u32[]{:S(2)}) copy-start(f32[256,128,32]{1,2,0:T(8,128)} %fusion.87) | copy-start | bytes 12582916
  160.7 5.3 %copy-start.1 = (f32[256,128,32]{1,0,2:T(8,128)S(1)}, f32[256,128,32]{1,0,2:T(8,128)}, u32[]{:S(2)}) copy-start(f32[256,128,32]{1,0,2:T(8,128)} %copy-done) | copy-start | bytes 12582916
  160.8 5.3 %copy-start.4 = (f32[256,128,32]{1,2,0:T(8,128)S(1)}, f32[256,128,32]{1,2,0:T(8,128)}, u32[]{:S(2)}) copy-start(f32[256,128,32]{1,2,0:T(8,128)} %fusion.18) | copy-start | bytes 12582916
  229.4 1.6 copy-start.6
  229.4 1.6 copy-start.13
  243.1 20.2 %copy-start.11 = (bf16[4096,128]{1,0:T(8,128)(2,1)S(1)}, bf16[4096,128]{1,0:T(8,128)(2,1)}, u32[]{:S(2)}) copy-start(bf16[4096,128]{1,0:T(8,128)(2,1)} %param.6) | copy-start | bytes 3145732
  257.3 31.0 %all-to-all-start.3 = ((bf16[16,2,16384]{2,1,0:T(2,128)(2,1)}), bf16[16,2,16384]{2,1,0:T(2,128)(2,1)}, u32[]{:S(2)}, u32[]{:S(2)}) async-start(bf16[16,2,16384]{2,1,0:T(2,128)(2,1)} %reshape.154), calls=%async_computation.3 | async-start | bytes 2097152 | tf_op jit(solution)/shard_map/all_to_all | solution.py:108
where the time goes:
time: 312 us; the launch traced here: 307 us
  matrix products  125 us (40%)
  local copies, waits for them, and re-layouts  55.5 us (18%)
  waiting for transfers between devices  46.6 us (15%)
  other arithmetic  34.2 us (11%)
  starting transfers between devices  26.3 us (8%)
  blocking collectives  18.4 us (6%)
    all_to_all x1, waiting for transfers between devices, local(): lax.all_to_all(mixed_out[None], 'context', split_axis=2, concat_axis=0, t...  24.9 us
    all_to_all x1, waiting for transfers between devices, local(): lax.all_to_all(products.reshape(context_size, local_channels, block_rows)...  21.7 us
    dot_general x2, matrix products, forward(): jnp.einsum('ckm,mj->ckj', turn_real, second_sin, precision=HIGHEST)  19.6 us
    all_gather x1, blocking collectives, local(): weights = lax.all_gather(short_filters, 'context', axis=2, tiled=True)  18.4 us
    dot_general x1, matrix products, causal_mix(): jnp.einsum('nk,ckm->cnm', first_cos[:half_rows, :], untwist_real, precisi...  17.6 us
    dot_general x1, matrix products, causal_mix(): jnp.einsum('nk,ckm->cnm', first_sin[:half_rows, :], untwist_imag, precisi...  17.6 us
    dot_general x2, matrix products, forward(): jnp.einsum('ckm,mj->ckj', turn_imag, second_cos, precision=HIGHEST)  16.8 us
    unnamed x35, local copies, waits for them, and re-layouts  16 us
  transfers between devices with their start and end apart: 5, of which 2 were waited for; matrix products, arithmetic and copies ran while one was open for 18% of the time, Pallas kernels for 0%

commit v1 on v0

--- a/solution.py
+++ b/solution.py
@@ -105,7 +105,12 @@
     arrived = arrived[0].astype(jnp.float32)
     convolved = causal_mix(arrived, filters)
     mixed_out = (convolved + skip_gain[:, None] * arrived).astype(jnp.bfloat16)
-    returned = lax.all_to_all(mixed_out[None], "context", split_axis=2, concat_axis=0, tiled=True)
+    returned = jnp.concatenate(
+        lax.all_to_all(
+            jnp.stack(jnp.split(mixed_out[None], lax.axis_size("context"), axis=2)), "context", 0, 0
+        ),
+        axis=0,
+    )
     returned = returned.reshape(group_width, block_rows)
     return (query_short * returned.astype(jnp.float32)).astype(jnp.bfloat16)
 

time: 312 us -> 287 us (0.920)
  other arithmetic: 34.2 us -> 21.3 us
  local copies, waits for them, and re-layouts: 55.5 us -> 43.1 us
    convert_element_type x1 -> x0, local copies, waits for them, and re-layouts: 11.7 us -> none  [local(): mixed_out = (convolved + skip_gain[:, None] * arrived).astype(jnp.bfloat16)]
    unnamed x1 -> x0, other arithmetic: 11.5 us -> none
    convert_element_type x2 -> x1, other arithmetic: 7.96 us -> 6.5 us  [local(): return (query_short * returned.astype(jnp.float32)).astype(jnp.bfloat16)]
    unnamed x35 -> x47, local copies, waits for them, and re-layouts: 16 us -> 17 us
  transfers between devices with their start and end apart: 5 -> 5, of which waited for: 2 -> 2; matrix products, arithmetic and copies ran while one was open for 18% -> 19% of each run, Pallas kernels for 0% -> 0%
where the time goes in v1:
time: 287 us; the launch traced here: 282 us
  matrix products  126 us (44%)
  waiting for transfers between devices  46.6 us (16%)
  local copies, waits for them, and re-layouts  43.1 us (15%)
  starting transfers between devices  26.1 us (9%)
  other arithmetic  21.3 us (7%)
  blocking collectives  18.4 us (6%)
    all_to_all x1, waiting for transfers between devices, local(): lax.all_to_all(jnp.stack(jnp.split(mixed_out[None], lax.axis_size('contex...  24.9 us
    all_to_all x1, waiting for transfers between devices, local(): lax.all_to_all(products.reshape(context_size, local_channels, block_rows)...  21.8 us
    dot_general x2, matrix products, forward(): jnp.einsum('ckm,mj->ckj', turn_real, second_sin, precision=HIGHEST)  19.9 us
    all_gather x1, blocking collectives, local(): weights = lax.all_gather(short_filters, 'context', axis=2, tiled=True)  18.4 us
    dot_general x1, matrix products, causal_mix(): jnp.einsum('nk,ckm->cnm', first_cos[:half_rows, :], untwist_real, precisi...  17.8 us
    dot_general x1, matrix products, causal_mix(): jnp.einsum('nk,ckm->cnm', first_sin[:half_rows, :], untwist_imag, precisi...  17.4 us
    dot_general x2, matrix products, forward(): jnp.einsum('ckm,mj->ckj', turn_imag, second_cos, precision=HIGHEST)  17.2 us
    unnamed x47, local copies, waits for them, and re-layouts  17 us
  transfers between devices with their start and end apart: 5, of which 2 were waited for; matrix products, arithmetic and copies ran while one was open for 19% of the time, Pallas kernels for 0%

profile of v1, /device:TPU:13, one launch (start us, length us, event | category | flops | bytes accessed | tf_op | source)
XLA Modules:
  0.0 282.2 jit_solution(7059127035740623546)
XLA Ops:
  11.7 4.6 %all-to-all-start.1 = ((bf16[64,2,16,256]{3,2,0,1:T(8,128)(2,1)}), bf16[64,2,16,256]{3,2,0,1:T(8,128)(2,1)}, u32[]{:S(2)}, u32[]{:S(2)}) async-start(bf16[64,2,16,256]{3,2,0,1:T(8,128)(2,1)} %copy.141), calls=%async_computation.1 | async-start | bytes 2097152 | tf_op jit(solution)/shard_map/all_to_all | solution.py:86
  16.3 18.4 %all_gather.3 = f32[3,3,4096]{2,1,0:T(4,128)S(1)} all-gather(f32[3,3,256]{2,1,0:T(4,128)S(1)} %copy-done.12), channel_id=1, replica_groups=mesh['tensor'=2,'context'=16] {'context'}, dimensions={2}, use_global_device_ids=true | all-gather | bytes 156672 | tf_op jit(solution)/shard_map/all_gather | solution.py:91
  42.7 7.9 %fusion.29 = bf16[4096,128]{1,0:T(8,128)(2,1)} fusion(f32[4096,2]{1,0:T(8,128)S(1)} %get-tuple-element.12, f32[4096,128]{1,0:T(8,128)S(1)} %copy-done.8, f32[4096,2]{1,0:T(8,128)S(1)} %get-tuple-element.11, f32[4096,128]{1,0:T(8,128)S(1)} %copy-done.7, f32[4096]{0:T(1024)S(1)} %bitcast.202, f32[4096]{0:T(1024)S(1)} %bitcast.203, f32[4096]{0:T(1024)S(1)} %bitcast.204, ...), kind=kLoop, calls=%fused_computation.43 | loop fusion | flops 8388608 | bytes 5406720 | tf_op jit(solution)/shard_map/convert_element_type | solution.py:97
  50.6 6.5 %all-to-all-start = ((bf16[16,256,128]{2,1,0:T(8,128)(2,1)}), bf16[16,256,128]{2,1,0:T(8,128)(2,1)S(1)}, u32[]{:S(2)}, u32[]{:S(2)}) async-start(bf16[16,256,128]{2,1,0:T(8,128)(2,1)} %bitcast.15), calls=%async_computation | async-start | bytes 2097152 | tf_op jit(solution)/shard_map/all_to_all | solution.py:98
  60.3 21.8 %all-to-all-done = bf16[16,256,128]{2,1,0:T(8,128)(2,1)S(1)} async-done(((bf16[16,256,128]{2,1,0:T(8,128)(2,1)}), bf16[16,256,128]{2,1,0:T(8,128)(2,1)S(1)}, u32[]{:S(2)}, u32[]{:S(2)}) %all-to-all-start) | async-done | bytes 1048608 | tf_op jit(solution)/shard_map/all_to_all | solution.py:98
  82.1 5.1 %all-to-all-start.2 = ((bf16[128,1,16,256]{3,0,1,2:T(8,128)(2,1)}), bf16[128,1,16,256]{3,0,1,2:T(8,128)(2,1)S(1)}, u32[]{:S(2)}, u32[]{:S(2)}) async-start(bf16[128,1,16,256]{3,0,1,2:T(8,128)(2,1)} %copy.142), calls=%async_computation.2 | async-start | bytes 2097152 | tf_op jit(solution)/shard_map/all_to_all | solution.py:87
  96.6 6.4 %fusion.12 = f32[256,128,32]{1,2,0:T(8,128)S(1)} fusion(f32[256,128,32]{1,0,2:T(8,128)S(1)} %get-tuple-element.10), kind=kOutput, calls=%fused_computation.28 | convolution fusion | flops 402668544 | bytes 8388608 | tf_op jit(solution)/shard_map/ckm,mj->ckj/dot_general | solution.py:53
  102.9 9.5 %fusion.10 = f32[256,128,32]{1,2,0:T(8,128)} fusion(f32[256,128,32]{1,0,2:T(8,128)S(1)} %get-tuple-element.10), kind=kOutput, calls=%fused_computation.26 | convolution fusion | flops 402667520 | bytes 8388608 | tf_op jit(solution)/shard_map/ckm,mj->ckj/dot_general | solution.py:56
  112.4 8.9 %fusion.18 = f32[256,128,32]{1,2,0:T(8,128)} fusion(f32[256,128,32]{1,2,0:T(8,128)S(1)} %fusion.12, f32[256,128,32]{1,0,2:T(8,128)S(1)} %get-tuple-element.9), kind=kOutput, calls=%fused_computation.34 | convolution fusion | flops 403716096 | bytes 12582912 | tf_op jit(solution)/shard_map/ckm,mj->ckj/dot_general | solution.py:53
  123.0 5.6 %add_bitcast_fusion = (f32[256,128,32]{0,1,2:T(8,128)}, f32[256,128,32]{0,1,2:T(8,128)}) fusion(f32[128,256,32]{1,0,2:T(8,128)S(1)} %fusion.51, f32[128,32]{0,1:T(8,128)S(1)} %get-tuple-element.23, f32[128,32]{0,1:T(8,128)S(1)} %get-tuple-element.24, bf16[256,64,32]{0,2,1:T(8,128)(2,1)S(1)} %bitcast.192, f32[128,128]{0,1:T(8,128)S(1)} %fusion.81), kind=kOutput, calls=%fused_computation.24 | convolution fusion | flops 408944640 | bytes 13697024 | tf_op jit(solution)/shard_map/kn,cnm->ckm/dot_general | solution.py:49
  128.6 5.6 %copy.146 = f32[256,128,32]{1,2,0:T(8,128)} copy(f32[256,128,32]{0,1,2:T(8,128)} %get-tuple-element.8) | data formatting | bytes 8388608 | tf_op jit(solution)/shard_map/sub | solution.py:51
  134.2 8.0 %fusion.92 = f32[256,128,32]{1,2,0:T(8,128)} fusion(f32[256,128,32]{1,2,0:T(8,128)} %copy.146), kind=kOutput, calls=%fused_computation.144 | convolution fusion | flops 402668544 | bytes 8388608 | tf_op jit(solution)/shard_map/ckm,mj->ckj/dot_general | solution.py:56
  142.3 5.4 %fusion.103 = f32[256,128,32]{1,2,0:T(8,128)} fusion(f32[256,128,32]{1,2,0:T(8,128)S(1)} %copy-done.3), kind=kOutput, calls=%fused_computation.155 | convolution fusion | flops 402667520 | bytes 8388608 | tf_op jit(solution)/shard_map/ckm,mj->ckj/dot_general | solution.py:53
  147.7 5.5 %copy.147 = f32[256,128,32]{1,2,0:T(8,128)} copy(f32[256,128,32]{0,1,2:T(8,128)} %get-tuple-element.7) | data formatting | bytes 8388608 | tf_op jit(solution)/shard_map/add | solution.py:52
  153.1 7.7 %convolution_add_fusion = f32[256,128,32]{1,2,0:T(8,128)S(1)} fusion(f32[256,128,32]{1,2,0:T(8,128)} %fusion.92, f32[256,128,32]{1,2,0:T(8,128)} %copy.147), kind=kOutput, calls=%fused_computation.36 | convolution fusion | flops 403716096 | bytes 12582912 | tf_op jit(solution)/shard_map/ckm,mj->ckj/dot_general | solution.py:56
  160.9 5.3 %convolution_subtract_fusion = f32[256,128,32]{1,2,0:T(8,128)} fusion(f32[256,128,32]{1,2,0:T(8,128)S(1)} %copy-done.5, f32[256,128,32]{1,2,0:T(8,128)S(1)} %copy-done.2), kind=kOutput, calls=%fused_computation.37 | convolution fusion | flops 403717120 | bytes 12582912 | tf_op jit(solution)/shard_map/ckm,mj->ckj/dot_general | solution.py:53
  166.2 11.8 %multiply_subtract_fusion = (f32[256,128,32]{1,2,0:T(8,128)S(1)}, f32[256,128,32]{1,2,0:T(8,128)S(1)}) fusion(f32[256,128,32]{1,2,0:T(8,128)S(1)} %convolution_add_fusion, f32[256,128,32]{1,2,0:T(8,128)S(1)} %copy-done.4, f32[256,128,32]{1,2,0:T(8,128)} %convolution_subtract_fusion, f32[256,128,32]{1,2,0:T(8,128)} %fusion.10, f32[256,128,32]{1,0,2:T(8,128)S(1)} %copy-done.1), kind=kOutput, calls=%fused_computation.23 | convolution fusion | flops 410008576 | bytes 29360128 | tf_op jit(solution)/shard_map/ckm,mj->ckj/dot_general | solution.py:56
  186.1 4.1 %fusion.88 = f32[256,128,32]{1,2,0:T(8,128)S(1)} fusion(f32[256,128,32]{1,2,0:T(8,128)S(1)} %get-tuple-element.5), kind=kOutput, calls=%fused_computation.140 | convolution fusion | flops 402668544 | bytes 8388608 | tf_op jit(solution)/shard_map/ckm,mj->ckj/dot_general | solution.py:68
  190.2 4.2 %fusion.99 = f32[256,128,32]{1,2,0:T(8,128)S(1)} fusion(f32[256,128,32]{1,2,0:T(8,128)S(1)} %get-tuple-element.5), kind=kOutput, calls=%fused_computation.151 | convolution fusion | flops 402667520 | bytes 8388608 | tf_op jit(solution)/shard_map/ckm,mj->ckj/dot_general | solution.py:65
  194.4 17.4 %fusion.2 = f32[256,32,64]{0,2,1:T(8,128)S(1)} fusion(f32[128,32]{0,1:T(8,128)S(1)} %get-tuple-element.23, f32[128,32]{0,1:T(8,128)S(1)} %get-tuple-element.24, f32[256,128,32]{1,2,0:T(8,128)S(1)} %fusion.90, f32[256,128,32]{1,2,0:T(8,128)S(1)} %fusion.99, f32[256,128,32]{1,2,0:T(8,128)S(1)} %fusion.88, f32[256,128,32]{1,2,0:T(8,128)S(1)} %fusion.97, ...), kind=kOutput, calls=%fused_computation.14 | convolution fusion | flops 810549248 | bytes 18972672 | tf_op jit(solution)/shard_map/nk,ckm->cnm/dot_general | solution.py:75
  211.9 17.8 %multiply_bitcast_fusion = f32[256,64,32]{0,1,2:T(8,128)S(1)} fusion(f32[256,32,64]{0,2,1:T(8,128)S(1)} %fusion.2, f32[128,32]{0,1:T(8,128)S(1)} %get-tuple-element.23, f32[128,32]{0,1:T(8,128)S(1)} %get-tuple-element.24, f32[256,128,32]{1,2,0:T(8,128)S(1)} %fusion.90, f32[256,128,32]{1,2,0:T(8,128)S(1)} %fusion.99, f32[256,128,32]{1,2,0:T(8,128)S(1)} %fusion.88, ...), kind=kOutput, calls=%fused_computation.66 | convolution fusion | flops 811597824 | bytes 21069824 | tf_op jit(solution)/shard_map/nk,ckm->cnm/dot_general | solution.py:73
  241.8 6.0 %all-to-all-start.3 = ((bf16[16,1,256,128]{2,3,1,0:T(8,128)(2,1)}), bf16[16,1,256,128]{2,3,1,0:T(8,128)(2,1)}, u32[]{:S(2)}, u32[]{:S(2)}) async-start(bf16[16,1,256,128]{2,3,1,0:T(8,128)(2,1)} %fusion.62), calls=%async_computation.3 | async-start | bytes 2097152 | tf_op jit(solution)/shard_map/all_to_all | solution.py:109
  248.0 24.9 %all-to-all-done.3 = bf16[16,1,256,128]{2,3,1,0:T(8,128)(2,1)} async-done(((bf16[16,1,256,128]{2,3,1,0:T(8,128)(2,1)}), bf16[16,1,256,128]{2,3,1,0:T(8,128)(2,1)}, u32[]{:S(2)}, u32[]{:S(2)}) %all-to-all-start.3) | async-done | bytes 1048608 | tf_op jit(solution)/shard_map/all_to_all | solution.py:109
  275.5 6.5 %fusion.39 = bf16[4096,128]{1,0:T(8,128)(2,1)} fusion(f32[4096,2]{1,0:T(8,128)} %get-tuple-element.13, f32[4096,128]{1,0:T(8,128)S(1)} %convert_element_type.118, f32[16,1,256,128]{3,2,0,1:T(8,128)} %copy.160, f32[4096]{0:T(1024)S(1)} %bitcast.200, f32[4096]{0:T(1024)S(1)} %bitcast.201, f32[4096]{0:T(1024)S(1)} %bitcast.199), kind=kLoop, calls=%fused_computation.53 | loop fusion | flops 4718592 | bytes 5324800 | tf_op jit(solution)/shard_map/convert_element_type | solution.py:115
  (77 shorter events, 56.6 us)
Async XLA Ops:
  0.0 3.1 %copy-start.10 = (bf16[4096,128]{1,0:T(8,128)(2,1)S(1)}, bf16[4096,128]{1,0:T(8,128)(2,1)}, u32[]{:S(2)}) copy-start(bf16[4096,128]{1,0:T(8,128)(2,1)} %param.8) | copy-start | bytes 3145732
  4.4 11.9 %copy-start.12 = (f32[3,3,256]{2,1,0:T(4,128)S(1)}, f32[3,3,256]{2,1,0:T(4,128)}, u32[]{:S(2)}) copy-start(f32[3,3,256]{2,1,0:T(4,128)} %param.10) | copy-start | bytes 27652
  5.3 29.5 %copy-start.9 = (bf16[4096,128]{1,0:T(8,128)(2,1)S(1)}, bf16[4096,128]{1,0:T(8,128)(2,1)}, u32[]{:S(2)}) copy-start(bf16[4096,128]{1,0:T(8,128)(2,1)} %param.7) | copy-start | bytes 3145732
  5.3 32.4 %collective-permute-start = (bf16[3,4096,2]{1,2,0:T(2,128)(2,1)S(1)}, bf16[3,4096,2]{1,2,0:T(2,128)(2,1)S(1)}, u32[]{:S(2)}, u32[]{:S(2)}) collective-permute-start(bf16[3,4096,2]{1,2,0:T(2,128)(2,1)S(1)} %pad_maximum_fusion.3), channel_id=1, source_target_pairs={{0,1},{1,2},{2,3},{3,4},{4,5},{5,6},{6,7},{7,8},{8,9},{9,10},{10,1... | collective-permute-start | bytes 147464 | tf_op jit(solution)/shard_map/ppermute | solution.py:15
  11.7 38.9 %all-to-all-start.1 = ((bf16[64,2,16,256]{3,2,0,1:T(8,128)(2,1)}), bf16[64,2,16,256]{3,2,0,1:T(8,128)(2,1)}, u32[]{:S(2)}, u32[]{:S(2)}) async-start(bf16[64,2,16,256]{3,2,0,1:T(8,128)(2,1)} %copy.141), calls=%async_computation.1 | async-start | bytes 2097152 | tf_op jit(solution)/shard_map/all_to_all | solution.py:86
  39.7 2.1 copy-start.7
  39.7 3.0 %copy-start.8 = (f32[4096,128]{1,0:T(8,128)S(1)}, f32[4096,128]{1,0:T(8,128)}, u32[]{:S(2)}) copy-start(f32[4096,128]{1,0:T(8,128)} %convert_element_type.121) | copy-start | bytes 6291460
  50.6 31.5 %all-to-all-start = ((bf16[16,256,128]{2,1,0:T(8,128)(2,1)}), bf16[16,256,128]{2,1,0:T(8,128)(2,1)S(1)}, u32[]{:S(2)}, u32[]{:S(2)}) async-start(bf16[16,256,128]{2,1,0:T(8,128)(2,1)} %bitcast.15), calls=%async_computation | async-start | bytes 2097152 | tf_op jit(solution)/shard_map/all_to_all | solution.py:98
  82.1 39.3 %all-to-all-start.2 = ((bf16[128,1,16,256]{3,0,1,2:T(8,128)(2,1)}), bf16[128,1,16,256]{3,0,1,2:T(8,128)(2,1)S(1)}, u32[]{:S(2)}, u32[]{:S(2)}) async-start(bf16[128,1,16,256]{3,0,1,2:T(8,128)(2,1)} %copy.142), calls=%async_computation.2 | async-start | bytes 2097152 | tf_op jit(solution)/shard_map/all_to_all | solution.py:87
  96.6 15.9 %copy-start = (f32[256,128,32]{1,0,2:T(8,128)}, f32[256,128,32]{1,0,2:T(8,128)S(1)}, u32[]{:S(2)}) copy-start(f32[256,128,32]{1,0,2:T(8,128)S(1)} %get-tuple-element.9) | copy-start | bytes 12582916
  134.2 8.1 %copy-start.3 = (f32[256,128,32]{1,2,0:T(8,128)S(1)}, f32[256,128,32]{1,2,0:T(8,128)}, u32[]{:S(2)}) copy-start(f32[256,128,32]{1,2,0:T(8,128)} %copy.146) | copy-start | bytes 12582916
  153.1 7.7 %copy-start.2 = (f32[256,128,32]{1,2,0:T(8,128)S(1)}, f32[256,128,32]{1,2,0:T(8,128)}, u32[]{:S(2)}) copy-start(f32[256,128,32]{1,2,0:T(8,128)} %copy.147) | copy-start | bytes 12582916
  153.1 7.7 %copy-start.5 = (f32[256,128,32]{1,2,0:T(8,128)S(1)}, f32[256,128,32]{1,2,0:T(8,128)}, u32[]{:S(2)}) copy-start(f32[256,128,32]{1,2,0:T(8,128)} %fusion.103) | copy-start | bytes 12582916
  160.9 5.3 %copy-start.1 = (f32[256,128,32]{1,0,2:T(8,128)S(1)}, f32[256,128,32]{1,0,2:T(8,128)}, u32[]{:S(2)}) copy-start(f32[256,128,32]{1,0,2:T(8,128)} %copy-done) | copy-start | bytes 12582916
  160.9 5.3 %copy-start.4 = (f32[256,128,32]{1,2,0:T(8,128)S(1)}, f32[256,128,32]{1,2,0:T(8,128)}, u32[]{:S(2)}) copy-start(f32[256,128,32]{1,2,0:T(8,128)} %fusion.18) | copy-start | bytes 12582916
  229.7 1.6 copy-start.6
  229.7 1.6 copy-start.13
  231.3 16.5 %copy-start.11 = (bf16[4096,128]{1,0:T(8,128)(2,1)S(1)}, bf16[4096,128]{1,0:T(8,128)(2,1)}, u32[]{:S(2)}) copy-start(bf16[4096,128]{1,0:T(8,128)(2,1)} %param.6) | copy-start | bytes 3145732
  241.8 31.0 %all-to-all-start.3 = ((bf16[16,1,256,128]{2,3,1,0:T(8,128)(2,1)}), bf16[16,1,256,128]{2,3,1,0:T(8,128)(2,1)}, u32[]{:S(2)}, u32[]{:S(2)}) async-start(bf16[16,1,256,128]{2,3,1,0:T(8,128)(2,1)} %fusion.62), calls=%async_computation.3 | async-start | bytes 2097152 | tf_op jit(solution)/shard_map/all_to_all | solution.py:109
